TPU v7x, 32 devices: a whole 2x2x4 slice. The times are simulated.
32 devices in a mesh: mem: 4 (over y, x), tile: 8 (over z, core).
Axes of the slice: x: 2, y: 2, z: 4, core: 2. Of those that a mesh axis runs over, the one named last changes fastest.
Arguments:
- ensemble: bfloat16 [32, 32, 128, 128], P('mem', None, 'tile'), may hold values from -0.75 to 0.75
- control: float32 [32, 16, 128, 128], P('mem', None, 'tile'), may hold values from -6 to 6
- level_loc: float32 [16, 16], replicated, may hold values from -0.35 to 1.25
- wind_speed: float32 [128, 128], P('tile'), may hold values from 0.1 to 0.35
- cell_codes: int32 [128, 128], P('tile'), may hold values from 0 to 2
- obs_cell: int32 [4096], P('tile'), may hold values from 0 to 2047
- innovation: float32 [32, 4096], P(None, 'tile'), may hold values from -12 to 12
- obs_sigma: float32 [32, 4096], P(None, 'tile'), may hold values from 0.5 to 2
Outputs:
- obs_gradient: float32 [32, 16, 128, 128], P('mem', None, 'tile')
Inputs may be any that keep to these rules, and one draw needn't show every extreme that they name: obs_cell[j] counts cells within tile j // 512, as (x - tile's first x) * 128 + y; several observations may share a cell. `cell_codes`: 0 is an open cell, 1 a wall cell that no flux enters or leaves, 2 an open cell that keeps 0.7 of its value each step.
All inputs are finite; a program needn't handle non-finite values.
Results may differ from a plain program's by a relative error of at most 0.0003.
Values may be sent and summed in bfloat16 or wider, within the bound.
A program may use at most 64 MiB of HBM per device.

v0:
```python
import jax
import jax.numpy as jnp
from jax import lax
from jax.sharding import PartitionSpec as P

L = 16
V = 2
STEPS = 2
VL = 32


diffusion_rate = 0.12
absorbing = 0.7
step_length = 0.5
huber_delta = 1.0


def with_halo(block, sides, width):
    for axis, dim in sides:
        count = lax.axis_size(axis)
        forward = [(i, i + 1) for i in range(count - 1)]
        backward = [(target, source) for source, target in forward]
        low = lax.ppermute(
            lax.slice_in_dim(block, block.shape[dim] - width, None, axis=dim), axis, forward
        )
        high = lax.ppermute(lax.slice_in_dim(block, 0, width, axis=dim), axis, backward)
        block = jnp.concatenate([low, block, high], axis=dim)
    return block


def smooth_padded(padded):
    along_x = 0.5 * padded[:, :, 1:-1] + 0.25 * (padded[:, :, :-2] + padded[:, :, 2:])
    y_padded = jnp.pad(along_x, ((0, 0), (0, 0), (0, 0), (1, 1)))
    return 0.5 * along_x + 0.25 * (y_padded[..., :-2] + y_padded[..., 2:])


def smooth_local(values):
    padded = with_halo(values, (("tile", 2),), 1)
    return smooth_padded(padded)


def apply_stencil(state_field, coeffs):
    center, west_coef, east_coef, south_coef, north_coef = coeffs
    padded = with_halo(state_field, (("tile", 1),), 1)
    y_padded = jnp.pad(state_field, ((0, 0), (0, 0), (1, 1)))
    return (
        center * state_field
        + west_coef * padded[:, :-2]
        + east_coef * padded[:, 2:]
        + south_coef * y_padded[:, :, :-2]
        + north_coef * y_padded[:, :, 2:]
    )


def body(ensemble, control, level_loc, wind_speed, cell_codes, obs_cell, innovation, obs_sigma):
    highest = lax.Precision.HIGHEST
    open_cells = (cell_codes != 1).astype(jnp.float32)
    absorb = jnp.where(cell_codes == 2, absorbing, 1.0).astype(jnp.float32)
    stacked = jnp.stack([open_cells, wind_speed])
    padded = with_halo(stacked, (("tile", 1),), 1)
    open_east = open_cells * padded[0, 2:]
    open_west = open_cells * padded[0, :-2]
    wind_west = padded[1, :-2]
    open_north = open_cells * jnp.pad(open_cells[:, 1:], ((0, 0), (0, 1)))
    open_south = open_cells * jnp.pad(open_cells[:, :-1], ((0, 0), (1, 0)))
    center = (
        1.0
        - diffusion_rate * (open_east + open_west + open_north + open_south)
        - wind_speed * open_east
    )
    forward = (
        center,
        (diffusion_rate + wind_west) * open_west,
        diffusion_rate * open_east,
        diffusion_rate * open_south,
        diffusion_rate * open_north,
    )
    adjoint = (
        center,
        diffusion_rate * open_west,
        (diffusion_rate + wind_speed) * open_east,
        diffusion_rate * open_south,
        diffusion_rate * open_north,
    )
    members = ensemble.shape[0]
    width_x = ensemble.shape[2]
    width_y = ensemble.shape[3]
    ens_split = ensemble.reshape(members, V, L, width_x, width_y)

    def evaluate(weights):
        level_mixed = jnp.einsum("ml,klxy->kmxy", level_loc, weights, precision=highest)
        mixed = smooth_local(level_mixed)
        partial_sum = jnp.sum(ens_split.astype(jnp.float32) * mixed[:, None], 0).reshape(
            VL, width_x, width_y
        )
        state_field = lax.psum_scatter(partial_sum, "mem", scatter_dimension=0, tiled=True)
        row_count = state_field.shape[0]
        first_row = lax.axis_index("mem") * row_count
        obs_values = lax.dynamic_slice_in_dim(innovation, first_row, row_count, 0)
        obs_scale = lax.dynamic_slice_in_dim(obs_sigma, first_row, row_count, 0)
        row_count = state_field.shape[0]
        for sweep_index in range(STEPS):
            state_field = absorb * apply_stencil(state_field, forward)
        sampled = jnp.take(state_field.reshape(row_count, width_x * width_y), obs_cell, axis=1)
        scaled = (sampled - obs_values) / obs_scale
        obs_weight = jnp.clip(scaled, -huber_delta, huber_delta) / obs_scale
        gridded = (
            jnp.zeros((row_count, width_x * width_y), jnp.float32).at[:, obs_cell].add(obs_weight)
        )
        adjoint_field = gridded.reshape(row_count, width_x, width_y)
        for sweep_index in range(STEPS):
            adjoint_field = apply_stencil(absorb * adjoint_field, adjoint)
        adjoint_field = lax.all_gather(adjoint_field, "mem", axis=0, tiled=True)
        adjoint_field = adjoint_field.reshape(V, L, width_x, width_y)
        member_term = jnp.sum(ens_split.astype(jnp.float32) * adjoint_field[None], 1)
        level_mix = jnp.einsum("ml,kmxy->klxy", level_loc, member_term, precision=highest)
        return smooth_local(level_mix)

    first = evaluate(control)
    next_control = control - step_length * (control + first)
    return evaluate(next_control)


def solution(mesh):
    placed = (
        P("mem", None, "tile", None),
        P("mem", None, "tile", None),
        P(),
        P("tile", None),
        P("tile", None),
        P("tile"),
        P(None, "tile"),
        P(None, "tile"),
    )
    return jax.shard_map(
        body, mesh=mesh, in_specs=placed, out_specs=P("mem", None, "tile", None), check_vma=False
    )
```

profile of v0, /device:TPU:1, one launch (start us, length us, event | category | flops | bytes accessed | tf_op | source)
XLA Modules:
  0.0 207.4 jit_solution(4653457017062749479)
XLA Ops:
  8.0 4.6 %collective-permute-start.1 = (f32[2,1,128]{2,1,0:T(1,128)S(1)}, f32[2,1,128]{2,1,0:T(1,128)S(1)}, u32[]{:S(2)}, u32[]{:S(2)}) collective-permute-start(f32[2,1,128]{2,1,0:T(1,128)S(1)} %get-tuple-element.38), channel_id=1, source_target_pairs={{0,1},{1,2},{2,3},{3,4},{4,5},{5,6},{6,7},{8,9},{9,10},{10,11},{11... | collective-permute-start | bytes 3080 | tf_op jit(solution)/shard_map/ppermute | solution.py:23
  14.5 2.5 %convolution_bitcast_fusion.3 = f32[8,16,16,128]{3,1,2,0:T(8,128)S(1)} fusion(f32[8,16,16,128]{3,2,1,0:T(8,128)} %param.11, f32[16,16]{1,0:T(8,128)S(1)} %copy-done), kind=kOutput, calls=%fused_computation.19 | convolution fusion | flops 50331648 | bytes 2098176 | tf_op jit(solution)/shard_map/ml,klxy->kmxy/dot_general | solution.py:91
  17.0 3.6 %collective-permute-start.2 = (f32[8,16,1,128]{3,1,2,0:T(8,128)S(1)}, f32[8,16,1,128]{3,1,2,0:T(8,128)S(1)}, u32[]{:S(2)}, u32[]{:S(2)}) collective-permute-start(f32[8,16,1,128]{3,1,2,0:T(8,128)S(1)} %get-tuple-element.16), channel_id=1, source_target_pairs={{0,1},{1,2},{2,3},{3,4},{4,5},{5,6},{6,7},{8,9},{9,10},{10,11},{11... | collective-permute-start | bytes 196616 | tf_op jit(solution)/shard_map/ppermute | solution.py:23
  22.7 3.6 %collective-permute-done.3 = f32[8,16,1,128]{3,1,2,0:T(8,128)S(1)} collective-permute-done((f32[8,16,1,128]{3,1,2,0:T(8,128)S(1)}, f32[8,16,1,128]{3,1,2,0:T(8,128)S(1)}, u32[]{:S(2)}, u32[]{:S(2)}) %collective-permute-start.3) | collective-permute-done | bytes 65568 | tf_op jit(solution)/shard_map/ppermute | solution.py:26
  29.8 23.4 %reduce-scatter.3.cloned.1.call-done = f32[8,16,128]{2,1,0:T(8,128)} async-done(((f32[32,16,128]{2,1,0:T(8,128)}), f32[8,16,128]{2,1,0:T(8,128)}) %reduce-scatter.3.cloned.1.call-update) | async-done | bytes 65552 | tf_op jit(solution)/shard_map/reduce_scatter | solution.py:96
  54.0 4.2 %collective-permute-start.4 = (f32[8,1,128]{2,1,0:T(1,128)S(1)}, f32[8,1,128]{2,1,0:T(1,128)S(1)}, u32[]{:S(2)}, u32[]{:S(2)}) collective-permute-start(f32[8,1,128]{2,1,0:T(1,128)S(1)} %get-tuple-element.32), channel_id=1, source_target_pairs={{0,1},{1,2},{2,3},{3,4},{4,5},{5,6},{6,7},{8,9},{9,10},{10,11},{11... | collective-permute-start | bytes 12296 | tf_op jit(solution)/shard_map/ppermute | solution.py:23
  60.3 2.9 %collective-permute-done.5 = f32[8,1,128]{2,1,0:T(1,128)S(1)} collective-permute-done((f32[8,1,128]{2,1,0:T(1,128)S(1)}, f32[8,1,128]{2,1,0:T(1,128)S(1)}, u32[]{:S(2)}, u32[]{:S(2)}) %collective-permute-start.5) | collective-permute-done | bytes 4128 | tf_op jit(solution)/shard_map/ppermute | solution.py:26
  66.3 2.4 %collective-permute-start.7 = (f32[8,1,128]{2,1,0:T(1,128)S(1)}, f32[8,1,128]{2,1,0:T(1,128)S(1)}, u32[]{:S(2)}, u32[]{:S(2)}) collective-permute-start(f32[8,1,128]{2,1,0:T(1,128)S(1)} %get-tuple-element.31), channel_id=1, source_target_pairs={{1,0},{2,1},{3,2},{4,3},{5,4},{6,5},{7,6},{9,8},{10,9},{11,10},{12... | collective-permute-start | bytes 12296 | tf_op jit(solution)/shard_map/ppermute | solution.py:26
  68.7 2.5 %collective-permute-done.7 = f32[8,1,128]{2,1,0:T(1,128)S(1)} collective-permute-done((f32[8,1,128]{2,1,0:T(1,128)S(1)}, f32[8,1,128]{2,1,0:T(1,128)S(1)}, u32[]{:S(2)}, u32[]{:S(2)}) %collective-permute-start.7) | collective-permute-done | bytes 4128 | tf_op jit(solution)/shard_map/ppermute | solution.py:26
  73.7 2.5 %scatter_custom_fusion = f32[8,2048]{0,1:T(8,128)S(1)} fusion(s32[512]{0:T(512)S(1)} %compare_select_fusion.1, f32[512,8]{1,0:T(8,128)S(1)} %copy.55, f32[]{:T(128)} %constant.7.clone.1), kind=kCustom, calls=%fused_computation.64 | custom fusion | flops 4096 | bytes 65540 | tf_op jit(solution)/shard_map/scatter-add | solution.py:108
  78.5 2.4 %collective-permute-start.9 = (f32[8,1,128]{2,1,0:T(1,128)S(1)}, f32[8,1,128]{2,1,0:T(1,128)S(1)}, u32[]{:S(2)}, u32[]{:S(2)}) collective-permute-start(f32[8,1,128]{2,1,0:T(1,128)S(1)} %get-tuple-element.29), channel_id=1, source_target_pairs={{1,0},{2,1},{3,2},{4,3},{5,4},{6,5},{7,6},{9,8},{10,9},{11,10},{12... | collective-permute-start | bytes 12296 | tf_op jit(solution)/shard_map/ppermute | solution.py:26
  80.9 2.5 %collective-permute-done.9 = f32[8,1,128]{2,1,0:T(1,128)S(1)} collective-permute-done((f32[8,1,128]{2,1,0:T(1,128)S(1)}, f32[8,1,128]{2,1,0:T(1,128)S(1)}, u32[]{:S(2)}, u32[]{:S(2)}) %collective-permute-start.9) | collective-permute-done | bytes 4128 | tf_op jit(solution)/shard_map/ppermute | solution.py:26
  85.5 2.4 %collective-permute-start.11 = (f32[8,1,128]{2,1,0:T(1,128)S(1)}, f32[8,1,128]{2,1,0:T(1,128)S(1)}, u32[]{:S(2)}, u32[]{:S(2)}) collective-permute-start(f32[8,1,128]{2,1,0:T(1,128)S(1)} %get-tuple-element.27), channel_id=1, source_target_pairs={{1,0},{2,1},{3,2},{4,3},{5,4},{6,5},{7,6},{9,8},{10,9},{11,10},{12... | collective-permute-start | bytes 12296 | tf_op jit(solution)/shard_map/ppermute | solution.py:26
  87.9 2.5 %collective-permute-done.11 = f32[8,1,128]{2,1,0:T(1,128)S(1)} collective-permute-done((f32[8,1,128]{2,1,0:T(1,128)S(1)}, f32[8,1,128]{2,1,0:T(1,128)S(1)}, u32[]{:S(2)}, u32[]{:S(2)}) %collective-permute-start.11) | collective-permute-done | bytes 4128 | tf_op jit(solution)/shard_map/ppermute | solution.py:26
  90.5 7.8 %all_gather.6 = f32[32,16,128]{2,1,0:T(8,128)S(1)} all-gather(f32[8,16,128]{2,1,0:T(8,128)S(1)} %fusion.56), channel_id=1, replica_groups=mesh['mem'=4,'tile'=8] {'mem'}, dimensions={0}, use_global_device_ids=true | all-gather | bytes 327680 | tf_op jit(solution)/shard_map/all_gather | solution.py:113
  100.0 3.5 %collective-permute-start.12 = (f32[8,16,1,128]{3,1,2,0:T(8,128)S(1)}, f32[8,16,1,128]{3,1,2,0:T(8,128)S(1)}, u32[]{:S(2)}, u32[]{:S(2)}) collective-permute-start(f32[8,16,1,128]{3,1,2,0:T(8,128)S(1)} %get-tuple-element.14), channel_id=1, source_target_pairs={{0,1},{1,2},{2,3},{3,4},{4,5},{5,6},{6,7},{8,9},{9,10},{10,11},{11... | collective-permute-start | bytes 196616 | tf_op jit(solution)/shard_map/ppermute | solution.py:23
  105.5 3.6 %collective-permute-done.13 = f32[8,16,1,128]{3,1,2,0:T(8,128)S(1)} collective-permute-done((f32[8,16,1,128]{3,1,2,0:T(8,128)S(1)}, f32[8,16,1,128]{3,1,2,0:T(8,128)S(1)}, u32[]{:S(2)}, u32[]{:S(2)}) %collective-permute-start.13) | collective-permute-done | bytes 65568 | tf_op jit(solution)/shard_map/ppermute | solution.py:26
  112.8 2.6 %collective-permute-start.15 = (f32[8,16,1,128]{3,1,2,0:T(8,128)S(1)}, f32[8,16,1,128]{3,1,2,0:T(8,128)S(1)}, u32[]{:S(2)}, u32[]{:S(2)}) collective-permute-start(f32[8,16,1,128]{3,1,2,0:T(8,128)S(1)} %get-tuple-element.13), channel_id=1, source_target_pairs={{1,0},{2,1},{3,2},{4,3},{5,4},{6,5},{7,6},{9,8},{10,9},{11,10},{12... | collective-permute-start | bytes 196616 | tf_op jit(solution)/shard_map/ppermute | solution.py:26
  115.4 3.0 %collective-permute-done.15 = f32[8,16,1,128]{3,1,2,0:T(8,128)S(1)} collective-permute-done((f32[8,16,1,128]{3,1,2,0:T(8,128)S(1)}, f32[8,16,1,128]{3,1,2,0:T(8,128)S(1)}, u32[]{:S(2)}, u32[]{:S(2)}) %collective-permute-start.15) | collective-permute-done | bytes 65568 | tf_op jit(solution)/shard_map/ppermute | solution.py:26
  120.7 22.1 %reduce-scatter.5.cloned.1.call-done = f32[8,16,128]{2,1,0:T(8,128)} async-done(((f32[32,16,128]{2,1,0:T(8,128)}), f32[8,16,128]{2,1,0:T(8,128)}) %reduce-scatter.5.cloned.1.call-update) | async-done | bytes 65552 | tf_op jit(solution)/shard_map/reduce_scatter | solution.py:96
  143.6 4.2 %collective-permute-start.16 = (f32[8,1,128]{2,1,0:T(1,128)S(1)}, f32[8,1,128]{2,1,0:T(1,128)S(1)}, u32[]{:S(2)}, u32[]{:S(2)}) collective-permute-start(f32[8,1,128]{2,1,0:T(1,128)S(1)} %get-tuple-element.24), channel_id=1, source_target_pairs={{0,1},{1,2},{2,3},{3,4},{4,5},{5,6},{6,7},{8,9},{9,10},{10,11},{11... | collective-permute-start | bytes 12296 | tf_op jit(solution)/shard_map/ppermute | solution.py:23
  149.7 3.0 %collective-permute-done.17 = f32[8,1,128]{2,1,0:T(1,128)S(1)} collective-permute-done((f32[8,1,128]{2,1,0:T(1,128)S(1)}, f32[8,1,128]{2,1,0:T(1,128)S(1)}, u32[]{:S(2)}, u32[]{:S(2)}) %collective-permute-start.17) | collective-permute-done | bytes 4128 | tf_op jit(solution)/shard_map/ppermute | solution.py:26
  155.8 2.4 %collective-permute-start.19 = (f32[8,1,128]{2,1,0:T(1,128)S(1)}, f32[8,1,128]{2,1,0:T(1,128)S(1)}, u32[]{:S(2)}, u32[]{:S(2)}) collective-permute-start(f32[8,1,128]{2,1,0:T(1,128)S(1)} %get-tuple-element.23), channel_id=1, source_target_pairs={{1,0},{2,1},{3,2},{4,3},{5,4},{6,5},{7,6},{9,8},{10,9},{11,10},{12... | collective-permute-start | bytes 12296 | tf_op jit(solution)/shard_map/ppermute | solution.py:26
  158.2 2.5 %collective-permute-done.19 = f32[8,1,128]{2,1,0:T(1,128)S(1)} collective-permute-done((f32[8,1,128]{2,1,0:T(1,128)S(1)}, f32[8,1,128]{2,1,0:T(1,128)S(1)}, u32[]{:S(2)}, u32[]{:S(2)}) %collective-permute-start.19) | collective-permute-done | bytes 4128 | tf_op jit(solution)/shard_map/ppermute | solution.py:26
  163.2 2.5 %scatter_custom_fusion.1 = f32[8,2048]{0,1:T(8,128)S(1)} fusion(s32[512]{0:T(512)S(1)} %compare_select_fusion.1, f32[512,8]{1,0:T(8,128)S(1)} %copy.64, f32[]{:T(128)} %constant.7.clone.1), kind=kCustom, calls=%fused_computation.62 | custom fusion | flops 4096 | bytes 65540 | tf_op jit(solution)/shard_map/scatter-add | solution.py:108
  168.0 2.4 %collective-permute-start.21 = (f32[8,1,128]{2,1,0:T(1,128)S(1)}, f32[8,1,128]{2,1,0:T(1,128)S(1)}, u32[]{:S(2)}, u32[]{:S(2)}) collective-permute-start(f32[8,1,128]{2,1,0:T(1,128)S(1)} %get-tuple-element.21), channel_id=1, source_target_pairs={{1,0},{2,1},{3,2},{4,3},{5,4},{6,5},{7,6},{9,8},{10,9},{11,10},{12... | collective-permute-start | bytes 12296 | tf_op jit(solution)/shard_map/ppermute | solution.py:26
  170.4 2.5 %collective-permute-done.21 = f32[8,1,128]{2,1,0:T(1,128)S(1)} collective-permute-done((f32[8,1,128]{2,1,0:T(1,128)S(1)}, f32[8,1,128]{2,1,0:T(1,128)S(1)}, u32[]{:S(2)}, u32[]{:S(2)}) %collective-permute-start.21) | collective-permute-done | bytes 4128 | tf_op jit(solution)/shard_map/ppermute | solution.py:26
  175.0 2.4 %collective-permute-start.23 = (f32[8,1,128]{2,1,0:T(1,128)S(1)}, f32[8,1,128]{2,1,0:T(1,128)S(1)}, u32[]{:S(2)}, u32[]{:S(2)}) collective-permute-start(f32[8,1,128]{2,1,0:T(1,128)S(1)} %get-tuple-element.19), channel_id=1, source_target_pairs={{1,0},{2,1},{3,2},{4,3},{5,4},{6,5},{7,6},{9,8},{10,9},{11,10},{12... | collective-permute-start | bytes 12296 | tf_op jit(solution)/shard_map/ppermute | solution.py:26
  177.4 2.5 %collective-permute-done.23 = f32[8,1,128]{2,1,0:T(1,128)S(1)} collective-permute-done((f32[8,1,128]{2,1,0:T(1,128)S(1)}, f32[8,1,128]{2,1,0:T(1,128)S(1)}, u32[]{:S(2)}, u32[]{:S(2)}) %collective-permute-start.23) | collective-permute-done | bytes 4128 | tf_op jit(solution)/shard_map/ppermute | solution.py:26
  180.0 7.8 %all_gather.7 = f32[32,16,128]{2,1,0:T(8,128)S(1)} all-gather(f32[8,16,128]{2,1,0:T(8,128)S(1)} %fusion.75), channel_id=1, replica_groups=mesh['mem'=4,'tile'=8] {'mem'}, dimensions={0}, use_global_device_ids=true | all-gather | bytes 327680 | tf_op jit(solution)/shard_map/all_gather | solution.py:113
  189.4 3.5 %collective-permute-start.24 = (f32[8,16,1,128]{3,1,2,0:T(8,128)S(1)}, f32[8,16,1,128]{3,1,2,0:T(8,128)S(1)}, u32[]{:S(2)}, u32[]{:S(2)}) collective-permute-start(f32[8,16,1,128]{3,1,2,0:T(8,128)S(1)} %get-tuple-element.10), channel_id=1, source_target_pairs={{0,1},{1,2},{2,3},{3,4},{4,5},{5,6},{6,7},{8,9},{9,10},{10,11},{11... | collective-permute-start | bytes 196616 | tf_op jit(solution)/shard_map/ppermute | solution.py:23
  194.9 3.6 %collective-permute-done.25 = f32[8,16,1,128]{3,1,2,0:T(8,128)S(1)} collective-permute-done((f32[8,16,1,128]{3,1,2,0:T(8,128)S(1)}, f32[8,16,1,128]{3,1,2,0:T(8,128)S(1)}, u32[]{:S(2)}, u32[]{:S(2)}) %collective-permute-start.25) | collective-permute-done | bytes 65568 | tf_op jit(solution)/shard_map/ppermute | solution.py:26
  (112 shorter events, 49.3 us)
Async XLA Ops:
  6.5 16.2 %copy-start.4 = (s32[16,128]{1,0:T(8,128)S(1)}, s32[16,128]{1,0:T(8,128)}, u32[]{:S(2)}) copy-start(s32[16,128]{1,0:T(8,128)} %param.14) | copy-start | bytes 24580
  6.5 46.7 %reduce-scatter.3.cloned.1.call-start = ((), (), s32[]{:S(2)}) async-start(), calls=%async_computation.2 | async-start | bytes 327680 | tf_op jit(solution)/shard_map/reduce_scatter | solution.py:96
  8.0 21.7 %collective-permute-start.1 = (f32[2,1,128]{2,1,0:T(1,128)S(1)}, f32[2,1,128]{2,1,0:T(1,128)S(1)}, u32[]{:S(2)}, u32[]{:S(2)}) collective-permute-start(f32[2,1,128]{2,1,0:T(1,128)S(1)} %get-tuple-element.38), channel_id=1, source_target_pairs={{0,1},{1,2},{2,3},{3,4},{4,5},{5,6},{6,7},{8,9},{9,10},{10,11},{11... | collective-permute-start | bytes 3080 | tf_op jit(solution)/shard_map/ppermute | solution.py:23
  12.6 17.1 %collective-permute-start = (f32[2,1,128]{2,1,0:T(1,128)S(1)}, f32[2,1,128]{2,1,0:T(1,128)S(1)}, u32[]{:S(2)}, u32[]{:S(2)}) collective-permute-start(f32[2,1,128]{2,1,0:T(1,128)S(1)} %get-tuple-element.39), channel_id=1, source_target_pairs={{1,0},{2,1},{3,2},{4,3},{5,4},{6,5},{7,6},{9,8},{10,9},{11,10},{12... | collective-permute-start | bytes 3080 | tf_op jit(solution)/shard_map/ppermute | solution.py:26
  17.0 5.7 %collective-permute-start.2 = (f32[8,16,1,128]{3,1,2,0:T(8,128)S(1)}, f32[8,16,1,128]{3,1,2,0:T(8,128)S(1)}, u32[]{:S(2)}, u32[]{:S(2)}) collective-permute-start(f32[8,16,1,128]{3,1,2,0:T(8,128)S(1)} %get-tuple-element.16), channel_id=1, source_target_pairs={{0,1},{1,2},{2,3},{3,4},{4,5},{5,6},{6,7},{8,9},{9,10},{10,11},{11... | collective-permute-start | bytes 196616 | tf_op jit(solution)/shard_map/ppermute | solution.py:23
  20.7 5.6 %collective-permute-start.3 = (f32[8,16,1,128]{3,1,2,0:T(8,128)S(1)}, f32[8,16,1,128]{3,1,2,0:T(8,128)S(1)}, u32[]{:S(2)}, u32[]{:S(2)}) collective-permute-start(f32[8,16,1,128]{3,1,2,0:T(8,128)S(1)} %get-tuple-element.17), channel_id=1, source_target_pairs={{1,0},{2,1},{3,2},{4,3},{5,4},{6,5},{7,6},{9,8},{10,9},{11,10},{12... | collective-permute-start | bytes 196616 | tf_op jit(solution)/shard_map/ppermute | solution.py:26
  28.6 44.2 %copy-start.5 = (f32[32,512]{1,0:T(8,128)S(1)}, f32[32,512]{1,0:T(8,128)}, u32[]{:S(2)}) copy-start(f32[32,512]{1,0:T(8,128)} %param.17) | copy-start | bytes 196612
  29.6 113.2 %reduce-scatter.5.cloned.1.call-start = ((), (), s32[]{:S(2)}) async-start(), calls=%async_computation.3 | async-start | bytes 327680 | tf_op jit(solution)/shard_map/reduce_scatter | solution.py:96
  29.7 46.8 %copy-start.7 = (pred[512]{0:T(512)(128)(4,1)}, pred[512]{0:T(512)(128)(4,1)S(1)}, u32[]{:S(2)}) copy-start(pred[512]{0:T(512)(128)(4,1)S(1)} %compare_and_fusion) | copy-start | bytes 1540
  54.0 6.2 %collective-permute-start.4 = (f32[8,1,128]{2,1,0:T(1,128)S(1)}, f32[8,1,128]{2,1,0:T(1,128)S(1)}, u32[]{:S(2)}, u32[]{:S(2)}) collective-permute-start(f32[8,1,128]{2,1,0:T(1,128)S(1)} %get-tuple-element.32), channel_id=1, source_target_pairs={{0,1},{1,2},{2,3},{3,4},{4,5},{5,6},{6,7},{8,9},{9,10},{10,11},{11... | collective-permute-start | bytes 12296 | tf_op jit(solution)/shard_map/ppermute | solution.py:23
  58.2 4.9 %collective-permute-start.5 = (f32[8,1,128]{2,1,0:T(1,128)S(1)}, f32[8,1,128]{2,1,0:T(1,128)S(1)}, u32[]{:S(2)}, u32[]{:S(2)}) collective-permute-start(f32[8,1,128]{2,1,0:T(1,128)S(1)} %get-tuple-element.33), channel_id=1, source_target_pairs={{1,0},{2,1},{3,2},{4,3},{5,4},{6,5},{7,6},{9,8},{10,9},{11,10},{12... | collective-permute-start | bytes 12296 | tf_op jit(solution)/shard_map/ppermute | solution.py:26
  64.3 4.4 %collective-permute-start.6 = (f32[8,1,128]{2,1,0:T(1,128)S(1)}, f32[8,1,128]{2,1,0:T(1,128)S(1)}, u32[]{:S(2)}, u32[]{:S(2)}) collective-permute-start(f32[8,1,128]{2,1,0:T(1,128)S(1)} %get-tuple-element.30), channel_id=1, source_target_pairs={{0,1},{1,2},{2,3},{3,4},{4,5},{5,6},{6,7},{8,9},{9,10},{10,11},{11... | collective-permute-start | bytes 12296 | tf_op jit(solution)/shard_map/ppermute | solution.py:23
  66.3 4.9 %collective-permute-start.7 = (f32[8,1,128]{2,1,0:T(1,128)S(1)}, f32[8,1,128]{2,1,0:T(1,128)S(1)}, u32[]{:S(2)}, u32[]{:S(2)}) collective-permute-start(f32[8,1,128]{2,1,0:T(1,128)S(1)} %get-tuple-element.31), channel_id=1, source_target_pairs={{1,0},{2,1},{3,2},{4,3},{5,4},{6,5},{7,6},{9,8},{10,9},{11,10},{12... | collective-permute-start | bytes 12296 | tf_op jit(solution)/shard_map/ppermute | solution.py:26
  76.5 4.3 %collective-permute-start.8 = (f32[8,1,128]{2,1,0:T(1,128)S(1)}, f32[8,1,128]{2,1,0:T(1,128)S(1)}, u32[]{:S(2)}, u32[]{:S(2)}) collective-permute-start(f32[8,1,128]{2,1,0:T(1,128)S(1)} %get-tuple-element.28), channel_id=1, source_target_pairs={{0,1},{1,2},{2,3},{3,4},{4,5},{5,6},{6,7},{8,9},{9,10},{10,11},{11... | collective-permute-start | bytes 12296 | tf_op jit(solution)/shard_map/ppermute | solution.py:23
  78.5 4.9 %collective-permute-start.9 = (f32[8,1,128]{2,1,0:T(1,128)S(1)}, f32[8,1,128]{2,1,0:T(1,128)S(1)}, u32[]{:S(2)}, u32[]{:S(2)}) collective-permute-start(f32[8,1,128]{2,1,0:T(1,128)S(1)} %get-tuple-element.29), channel_id=1, source_target_pairs={{1,0},{2,1},{3,2},{4,3},{5,4},{6,5},{7,6},{9,8},{10,9},{11,10},{12... | collective-permute-start | bytes 12296 | tf_op jit(solution)/shard_map/ppermute | solution.py:26
  83.5 4.3 %collective-permute-start.10 = (f32[8,1,128]{2,1,0:T(1,128)S(1)}, f32[8,1,128]{2,1,0:T(1,128)S(1)}, u32[]{:S(2)}, u32[]{:S(2)}) collective-permute-start(f32[8,1,128]{2,1,0:T(1,128)S(1)} %get-tuple-element.26), channel_id=1, source_target_pairs={{0,1},{1,2},{2,3},{3,4},{4,5},{5,6},{6,7},{8,9},{9,10},{10,11},{11... | collective-permute-start | bytes 12296 | tf_op jit(solution)/shard_map/ppermute | solution.py:23
  85.5 4.9 %collective-permute-start.11 = (f32[8,1,128]{2,1,0:T(1,128)S(1)}, f32[8,1,128]{2,1,0:T(1,128)S(1)}, u32[]{:S(2)}, u32[]{:S(2)}) collective-permute-start(f32[8,1,128]{2,1,0:T(1,128)S(1)} %get-tuple-element.27), channel_id=1, source_target_pairs={{1,0},{2,1},{3,2},{4,3},{5,4},{6,5},{7,6},{9,8},{10,9},{11,10},{12... | collective-permute-start | bytes 12296 | tf_op jit(solution)/shard_map/ppermute | solution.py:26
  100.0 5.5 %collective-permute-start.12 = (f32[8,16,1,128]{3,1,2,0:T(8,128)S(1)}, f32[8,16,1,128]{3,1,2,0:T(8,128)S(1)}, u32[]{:S(2)}, u32[]{:S(2)}) collective-permute-start(f32[8,16,1,128]{3,1,2,0:T(8,128)S(1)} %get-tuple-element.14), channel_id=1, source_target_pairs={{0,1},{1,2},{2,3},{3,4},{4,5},{5,6},{6,7},{8,9},{9,10},{10,11},{11... | collective-permute-start | bytes 196616 | tf_op jit(solution)/shard_map/ppermute | solution.py:23
  103.5 5.6 %collective-permute-start.13 = (f32[8,16,1,128]{3,1,2,0:T(8,128)S(1)}, f32[8,16,1,128]{3,1,2,0:T(8,128)S(1)}, u32[]{:S(2)}, u32[]{:S(2)}) collective-permute-start(f32[8,16,1,128]{3,1,2,0:T(8,128)S(1)} %get-tuple-element.15), channel_id=1, source_target_pairs={{1,0},{2,1},{3,2},{4,3},{5,4},{6,5},{7,6},{9,8},{10,9},{11,10},{12... | collective-permute-start | bytes 196616 | tf_op jit(solution)/shard_map/ppermute | solution.py:26
  110.9 4.5 %collective-permute-start.14 = (f32[8,16,1,128]{3,1,2,0:T(8,128)S(1)}, f32[8,16,1,128]{3,1,2,0:T(8,128)S(1)}, u32[]{:S(2)}, u32[]{:S(2)}) collective-permute-start(f32[8,16,1,128]{3,1,2,0:T(8,128)S(1)} %get-tuple-element.12), channel_id=1, source_target_pairs={{0,1},{1,2},{2,3},{3,4},{4,5},{5,6},{6,7},{8,9},{9,10},{10,11},{11... | collective-permute-start | bytes 196616 | tf_op jit(solution)/shard_map/ppermute | solution.py:23
  112.8 5.6 %collective-permute-start.15 = (f32[8,16,1,128]{3,1,2,0:T(8,128)S(1)}, f32[8,16,1,128]{3,1,2,0:T(8,128)S(1)}, u32[]{:S(2)}, u32[]{:S(2)}) collective-permute-start(f32[8,16,1,128]{3,1,2,0:T(8,128)S(1)} %get-tuple-element.13), channel_id=1, source_target_pairs={{1,0},{2,1},{3,2},{4,3},{5,4},{6,5},{7,6},{9,8},{10,9},{11,10},{12... | collective-permute-start | bytes 196616 | tf_op jit(solution)/shard_map/ppermute | solution.py:26
  120.7 41.6 %copy-start.8 = (pred[512]{0:T(512)(128)(4,1)S(1)}, pred[512]{0:T(512)(128)(4,1)}, u32[]{:S(2)}) copy-start(pred[512]{0:T(512)(128)(4,1)} %copy-done.7) | copy-start | bytes 1540
  143.6 6.1 %collective-permute-start.16 = (f32[8,1,128]{2,1,0:T(1,128)S(1)}, f32[8,1,128]{2,1,0:T(1,128)S(1)}, u32[]{:S(2)}, u32[]{:S(2)}) collective-permute-start(f32[8,1,128]{2,1,0:T(1,128)S(1)} %get-tuple-element.24), channel_id=1, source_target_pairs={{0,1},{1,2},{2,3},{3,4},{4,5},{5,6},{6,7},{8,9},{9,10},{10,11},{11... | collective-permute-start | bytes 12296 | tf_op jit(solution)/shard_map/ppermute | solution.py:23
  147.8 4.9 %collective-permute-start.17 = (f32[8,1,128]{2,1,0:T(1,128)S(1)}, f32[8,1,128]{2,1,0:T(1,128)S(1)}, u32[]{:S(2)}, u32[]{:S(2)}) collective-permute-start(f32[8,1,128]{2,1,0:T(1,128)S(1)} %get-tuple-element.25), channel_id=1, source_target_pairs={{1,0},{2,1},{3,2},{4,3},{5,4},{6,5},{7,6},{9,8},{10,9},{11,10},{12... | collective-permute-start | bytes 12296 | tf_op jit(solution)/shard_map/ppermute | solution.py:26
  153.8 4.3 %collective-permute-start.18 = (f32[8,1,128]{2,1,0:T(1,128)S(1)}, f32[8,1,128]{2,1,0:T(1,128)S(1)}, u32[]{:S(2)}, u32[]{:S(2)}) collective-permute-start(f32[8,1,128]{2,1,0:T(1,128)S(1)} %get-tuple-element.22), channel_id=1, source_target_pairs={{0,1},{1,2},{2,3},{3,4},{4,5},{5,6},{6,7},{8,9},{9,10},{10,11},{11... | collective-permute-start | bytes 12296 | tf_op jit(solution)/shard_map/ppermute | solution.py:23
  155.8 4.9 %collective-permute-start.19 = (f32[8,1,128]{2,1,0:T(1,128)S(1)}, f32[8,1,128]{2,1,0:T(1,128)S(1)}, u32[]{:S(2)}, u32[]{:S(2)}) collective-permute-start(f32[8,1,128]{2,1,0:T(1,128)S(1)} %get-tuple-element.23), channel_id=1, source_target_pairs={{1,0},{2,1},{3,2},{4,3},{5,4},{6,5},{7,6},{9,8},{10,9},{11,10},{12... | collective-permute-start | bytes 12296 | tf_op jit(solution)/shard_map/ppermute | solution.py:26
  166.1 4.3 %collective-permute-start.20 = (f32[8,1,128]{2,1,0:T(1,128)S(1)}, f32[8,1,128]{2,1,0:T(1,128)S(1)}, u32[]{:S(2)}, u32[]{:S(2)}) collective-permute-start(f32[8,1,128]{2,1,0:T(1,128)S(1)} %get-tuple-element.20), channel_id=1, source_target_pairs={{0,1},{1,2},{2,3},{3,4},{4,5},{5,6},{6,7},{8,9},{9,10},{10,11},{11... | collective-permute-start | bytes 12296 | tf_op jit(solution)/shard_map/ppermute | solution.py:23
  168.0 4.9 %collective-permute-start.21 = (f32[8,1,128]{2,1,0:T(1,128)S(1)}, f32[8,1,128]{2,1,0:T(1,128)S(1)}, u32[]{:S(2)}, u32[]{:S(2)}) collective-permute-start(f32[8,1,128]{2,1,0:T(1,128)S(1)} %get-tuple-element.21), channel_id=1, source_target_pairs={{1,0},{2,1},{3,2},{4,3},{5,4},{6,5},{7,6},{9,8},{10,9},{11,10},{12... | collective-permute-start | bytes 12296 | tf_op jit(solution)/shard_map/ppermute | solution.py:26
  173.1 4.3 %collective-permute-start.22 = (f32[8,1,128]{2,1,0:T(1,128)S(1)}, f32[8,1,128]{2,1,0:T(1,128)S(1)}, u32[]{:S(2)}, u32[]{:S(2)}) collective-permute-start(f32[8,1,128]{2,1,0:T(1,128)S(1)} %get-tuple-element.18), channel_id=1, source_target_pairs={{0,1},{1,2},{2,3},{3,4},{4,5},{5,6},{6,7},{8,9},{9,10},{10,11},{11... | collective-permute-start | bytes 12296 | tf_op jit(solution)/shard_map/ppermute | solution.py:23
  175.0 4.9 %collective-permute-start.23 = (f32[8,1,128]{2,1,0:T(1,128)S(1)}, f32[8,1,128]{2,1,0:T(1,128)S(1)}, u32[]{:S(2)}, u32[]{:S(2)}) collective-permute-start(f32[8,1,128]{2,1,0:T(1,128)S(1)} %get-tuple-element.19), channel_id=1, source_target_pairs={{1,0},{2,1},{3,2},{4,3},{5,4},{6,5},{7,6},{9,8},{10,9},{11,10},{12... | collective-permute-start | bytes 12296 | tf_op jit(solution)/shard_map/ppermute | solution.py:26
  189.4 5.5 %collective-permute-start.24 = (f32[8,16,1,128]{3,1,2,0:T(8,128)S(1)}, f32[8,16,1,128]{3,1,2,0:T(8,128)S(1)}, u32[]{:S(2)}, u32[]{:S(2)}) collective-permute-start(f32[8,16,1,128]{3,1,2,0:T(8,128)S(1)} %get-tuple-element.10), channel_id=1, source_target_pairs={{0,1},{1,2},{2,3},{3,4},{4,5},{5,6},{6,7},{8,9},{9,10},{10,11},{11... | collective-permute-start | bytes 196616 | tf_op jit(solution)/shard_map/ppermute | solution.py:23
  193.0 5.6 %collective-permute-start.25 = (f32[8,16,1,128]{3,1,2,0:T(8,128)S(1)}, f32[8,16,1,128]{3,1,2,0:T(8,128)S(1)}, u32[]{:S(2)}, u32[]{:S(2)}) collective-permute-start(f32[8,16,1,128]{3,1,2,0:T(8,128)S(1)} %get-tuple-element.11), channel_id=1, source_target_pairs={{1,0},{2,1},{3,2},{4,3},{5,4},{6,5},{7,6},{9,8},{10,9},{11,10},{12... | collective-permute-start | bytes 196616 | tf_op jit(solution)/shard_map/ppermute | solution.py:26
  (5 other events, 24.0 us)
Sparse Core Ops, SparseCore 0:
  29.7 23.4 reduce-scatter.2
  120.8 21.9 reduce-scatter.4
where the time goes:
time: 209 us; the launch traced here: 207 us
  waiting for transfers between devices  80.5 us (39%)
  starting transfers between devices  65.7 us (31%)
  other arithmetic  16.1 us (8%)
  blocking collectives  15.5 us (7%)
  between operations  14.1 us (7%)
  local copies, waits for them, and re-layouts  8.85 us (4%)
  matrix products  6.61 us (3%)
    reduce_scatter x2, waiting for transfers between devices, evaluate(): lax.psum_scatter(partial_sum, 'mem', scatter_dimension=0, tiled=True)  45.5 us
    ppermute x13, starting transfers between devices, with_halo(): lax.ppermute(lax.slice_in_dim(block, block.shape[dim] - width, None, axis...  37.3 us
    ppermute x13, waiting for transfers between devices, with_halo(): lax.ppermute(lax.slice_in_dim(block, 0, width, axis=dim), axis, backward)  34.9 us
    ppermute x13, starting transfers between devices, with_halo(): lax.ppermute(lax.slice_in_dim(block, 0, width, axis=dim), axis, backward)  28.3 us
    all_gather x2, blocking collectives, evaluate(): adjoint_field = lax.all_gather(adjoint_field, 'mem', axis=0, tiled=True)  15.5 us
    scatter-add x2, other arithmetic, evaluate(): jnp.zeros((row_count, width_x * width_y), jnp.float32).at[:, obs_cell]  5.01 us
  transfers between devices with their start and end apart: 28, of which 14 were waited for; matrix products, arithmetic and copies ran while one was open for 2% of the time, Pallas kernels for 0%

commit v1 on v0

v1 whole, which is shorter than its diff:
```python
import functools

import jax
import jax.numpy as jnp
from jax import lax
from jax.experimental import pallas as pl
from jax.experimental.pallas import tpu as pltpu
from jax.sharding import PartitionSpec as P

V = 2
STEPS = 2
HALO = 8

diffusion_rate = 0.12
absorbing = 0.7
step_length = 0.5
huber_delta = 1.0

MESH = pl.DeviceIdType.MESH
F32 = jnp.float32
BF16 = jnp.bfloat16
HIGHEST = lax.Precision.HIGHEST
NT = (((1,), (1,)), ((), ()))


def log2(n):
    assert n & (n - 1) == 0
    return n.bit_length() - 1


def iota(shape, dim):
    return lax.broadcasted_iota(jnp.int32, shape, dim)


def split(x):
    hi = x.astype(BF16)
    return hi, (x - hi.astype(F32)).astype(BF16)


def mm(a, b):
    return jnp.dot(a, b, preferred_element_type=F32)


def dot3(a, b):
    ah, al = a
    bh, bl = split(b)
    return mm(ah, bh) + (mm(ah, bl) + mm(al, bh))


def kernel(
    n_mem, n_tile, members, levels, width, ny, nobs,
    ens, ctl, loc, wind, codes, cell, innov, sigma,
    out,
    ensf, work, nxt, mats, small,
    ctl_stage, ctl_halo, codes_halo, wind_halo, cell_halo, innov_halo, sigma_halo,
    ens_stage, ens_halo,
    part, rs_buf, inc, inc_halo, ext, adj_stage, ag, edge_stage, agh,
    r0_send, r0_recv, rs_send, rs_recv, h_send, h_recv, ag_send, ag_recv, e_send, e_recv,
):
    m = lax.axis_index("mem")
    t = lax.axis_index("tile")
    has = (t > 0, t < n_tile - 1)
    rows = V * levels
    share = rows // n_mem
    block = levels * width
    xs = log2(width)

    def tell(dev):
        pl.semaphore_signal(pltpu.get_barrier_semaphore(), inc=1, device_id=dev, device_id_type=MESH)

    for d in range(1, n_mem):
        tell((lax.rem(m + d, n_mem), t))

    @pl.when(has[0])
    def _():
        tell((m, t - 1))

    @pl.when(has[1])
    def _():
        tell((m, t + 1))

    kl = members * levels
    ctl_stage[0] = ctl[pl.ds(width - 1, kl, stride=width), :]
    ctl_stage[1] = ctl[pl.ds(0, kl, stride=width), :]

    peers = n_mem - 1 + jnp.where(t > 0, 1, 0) + jnp.where(t < n_tile - 1, 1, 0)
    pl.semaphore_wait(pltpu.get_barrier_semaphore(), peers)

    def to_side(side, src, dst, ssem, rsem):
        dev = (m, t + 1) if side == 0 else (m, t - 1)
        return pltpu.make_async_remote_copy(
            src_ref=src, dst_ref=dst, send_sem=ssem, recv_sem=rsem, device_id=dev, device_id_type=MESH
        )

    mine = pl.ds(m * share, share)
    near = (pl.ds(width - HALO, HALO), pl.ds(0, HALO))
    first_msgs = []
    for side in (0, 1):
        pairs = [
            (ctl_stage.at[side], ctl_halo.at[side]),
            (codes.at[near[side]], codes_halo.at[side]),
            (wind.at[near[side]], wind_halo.at[side]),
            (cell, cell_halo.at[side]),
            (innov.at[m], innov_halo.at[side]),
            (sigma.at[m], sigma_halo.at[side]),
            (ens_stage.at[side], ens_halo.at[side]),
        ]
        first_msgs.append(
            [to_side(side, s, d, r0_send.at[side, i], r0_recv.at[side, i]) for i, (s, d) in enumerate(pairs)]
        )

    def start_side(side, which):
        @pl.when(has[1 - side])
        def _():
            for i in which:
                first_msgs[side][i].start()

    def recv_side(side, which):
        @pl.when(has[side])
        def _():
            for i in which:
                first_msgs[side][i].wait_recv()

    for side in (0, 1):
        start_side(side, (0,))
    for side in (0, 1):
        start_side(side, (1, 2, 3, 4, 5))

        @pl.when(jnp.logical_not(has[side]))
        def _():
            ctl_halo[side] = jnp.zeros_like(ctl_halo[side])
            codes_halo[side] = jnp.ones_like(codes_halo[side])
            wind_halo[side] = jnp.zeros_like(wind_halo[side])
            cell_halo[side] = jnp.full_like(cell_halo[side], -1)
            innov_halo[side] = jnp.zeros_like(innov_halo[side])
            sigma_halo[side] = jnp.ones_like(sigma_halo[side])
            ens_halo[side] = jnp.zeros_like(ens_halo[side])
            for e in (0, 1):
                inc_halo[e, side] = jnp.zeros_like(inc_halo[e, side])

    lo = loc[...]
    pick = (iota((block, levels), 0) >> xs == iota((block, levels), 1)).astype(F32)
    xr, xc = iota((block, block), 0) & (width - 1), iota((block, block), 1) & (width - 1)
    near_x = jnp.where(xr == xc, 0.5, jnp.where(jnp.abs(xr - xc) == 1, 0.25, 0.0)).astype(F32)
    ls = log2(levels)
    pick2 = ((iota((kl, levels), 0) & (levels - 1)) == iota((kl, levels), 1)).astype(F32)
    same_k = ((iota((kl, kl), 0) >> ls) == (iota((kl, kl), 1) >> ls)).astype(F32)

    def nt(a, b):
        return lax.dot_general(a, b, NT, precision=HIGHEST, preferred_element_type=F32)

    for i in (0, 1):
        def left(p):
            return jnp.dot(p, lo, precision=HIGHEST, preferred_element_type=F32) if i == 0 else nt(p, lo)

        hi, low = split(nt(left(pick), pick) * near_x)
        mats[i, 0] = hi
        mats[i, 1] = low
        hi, low = split(nt(left(pick2), pick2) * same_k)
        small[i, 0] = hi
        small[i, 1] = low

    yi = iota((1, ny), 1)
    from_south = jnp.where(yi > 0, 0.25, 0.0).astype(F32)
    from_north = jnp.where(yi < ny - 1, 0.25, 0.0).astype(F32)

    def smooth_y(v):
        return 0.5 * v + (from_south * pltpu.roll(v, 1, 1) + from_north * pltpu.roll(v, ny - 1, 1))

    def mix(src, i, edges):
        big = (mats[i, 0], mats[i, 1])
        for k in range(0, members, 2):
            both = jnp.concatenate(
                [src[k * block:(k + 1) * block, :], src[(k + 1) * block:(k + 2) * block, :]], axis=1
            )
            done = dot3(big, both)
            work[k * block:(k + 1) * block, :] = done[:, :ny]
            work[(k + 1) * block:(k + 2) * block, :] = done[:, ny:]
        side = dot3((small[i, 0], small[i, 1]), jnp.concatenate(edges(), axis=1))
        for j, x in ((0, 0), (1, width - 1)):
            at = pl.ds(x, kl, stride=width)
            work[at, :] = work[at, :] + 0.25 * side[:, j * ny:(j + 1) * ny]
        return side

    def send_mem(d, src, dst, ssem, rsem):
        return pltpu.make_async_remote_copy(
            src_ref=src, dst_ref=dst, send_sem=ssem, recv_sem=rsem,
            device_id=(lax.rem(m + d, n_mem), t), device_id_type=MESH,
        )

    def coefficients():
        code = jnp.concatenate([codes_halo[0], codes[...], codes_halo[1]], axis=0)
        speed = jnp.concatenate([wind_halo[0], wind[...], wind_halo[1]], axis=0)
        n = code.shape[0]
        opened = (code != 1).astype(F32)
        absorb = jnp.where(code == 2, absorbing, 1.0).astype(F32)
        yy = iota(code.shape, 1)
        oe = opened * pltpu.roll(opened, n - 1, 0)
        ow = opened * pltpu.roll(opened, 1, 0)
        on = jnp.where(yy < ny - 1, opened * pltpu.roll(opened, ny - 1, 1), 0.0)
        os = jnp.where(yy > 0, opened * pltpu.roll(opened, 1, 1), 0.0)
        k = diffusion_rate
        center = 1.0 - k * (oe + ow + on + os) - speed * oe
        fwd = (center, (k + pltpu.roll(speed, 1, 0)) * ow, k * oe, k * os, k * on)
        adj = (center, k * ow, (k + speed) * oe, k * os, k * on)
        return absorb, fwd, adj

    def stencil(q, coef):
        center, west, east, south, north = coef
        n = q.shape[0]
        return (
            center * q
            + west * pltpu.roll(q, 1, 0)
            + east * pltpu.roll(q, n - 1, 0)
            + south * pltpu.roll(q, 1, 1)
            + north * pltpu.roll(q, ny - 1, 1)
        )

    def observe(field, e):
        state = jnp.stack(field, axis=0)
        tiles = (
            (cell_halo[0], innov_halo[0], sigma_halo[0], 0, HALO, width - HALO),
            (cell[...], innov[m], sigma[m], HALO, width, 0),
            (cell_halo[1], innov_halo[1], sigma_halo[1], HALO + width, HALO, 0),
        )
        pieces = []
        for where, seen, dev, at, count, offset in tiles:
            hot_y = (iota((ny, nobs), 0) == (where & (ny - 1))).astype(BF16)
            hot_x = (iota((count, nobs), 0) == ((where >> log2(ny)) - offset)).astype(F32)
            part_state = state[:, at:at + count, :].reshape(share * count, ny)
            hi, low = split(part_state)
            got = (mm(hi, hot_y) + mm(low, hot_y)).reshape(share, count, nobs)
            sampled = jnp.sum(got * hot_x[None], axis=1)
            scaled = (sampled - seen) / dev
            weight = jnp.clip(scaled, -huber_delta, huber_delta) / dev
            hi, low = split(weight)
            total = None
            for w in (hi, low):
                spread = (w.astype(F32)[:, None, :] * hot_x[None]).reshape(share * count, nobs).astype(BF16)
                put = lax.dot_general(spread, hot_y, NT, preferred_element_type=F32)
                total = put if total is None else total + put
            pieces.append(total.reshape(share, count, ny))
        return jnp.concatenate(pieces, axis=1)


    def evaluate(e, src, edges):
        mix(src, 0, edges)
        for k in range(members):
            at = pl.ds(k * block, block)
            work[at, :] = smooth_y(work[at, :])
        copies = []
        for d in list(range(1, n_mem)) + [0]:
            who = lax.rem(m + d, n_mem)
            r0 = who * share
            l0 = lax.rem(r0, levels)
            total = jnp.zeros((share, width, ny), F32)
            for k in range(members):
                a = work[pl.ds(pl.multiple_of(k * block + l0 * width, width), share * width), :]
                total += ens[k, pl.ds(r0, share)].astype(F32) * a.reshape(share, width, ny)
            part[e, d] = total
            if d:
                copy = send_mem(d, part.at[e, d], rs_buf.at[e, d], rs_send.at[e, d], rs_recv.at[e, d])
                copy.start()
                copies.append(copy)
        if e == 0:
            for k in range(members):
                ensf[pl.ds(k * rows * width, rows * width), :] = (
                    ens[k].astype(F32).reshape(rows * width, ny)
                )
            for i in (0, 1):
                ens_stage[0, i] = ensf[pl.ds(width - 2 + i, members * rows, stride=width), :].astype(BF16)
                ens_stage[1, i] = ensf[pl.ds(i, members * rows, stride=width), :].astype(BF16)
            for side in (0, 1):
                start_side(side, (6,))
            for side in (0, 1):
                recv_side(side, (1, 2, 3, 4, 5))
        for copy in copies:
            copy.wait_recv()
        total = part[e, 0]
        for d in range(1, n_mem):
            total = total + rs_buf[e, d]
        inc[e, 0] = total[:, width - HALO:, :]
        inc[e, 1] = total[:, :HALO, :]
        halo = [
            to_side(side, inc.at[e, side], inc_halo.at[e, side], h_send.at[e, side], h_recv.at[e, side])
            for side in (0, 1)
        ]
        for side in (0, 1):
            @pl.when(has[1 - side])
            def _():
                halo[side].start()
        absorb, fwd, adj = coefficients()
        for side in (0, 1):
            @pl.when(has[side])
            def _():
                halo[side].wait_recv()
        whole = jnp.concatenate([inc_halo[e, 0], total, inc_halo[e, 1]], axis=1)
        n = HALO + width + HALO
        fields = [whole[r] for r in range(share)]
        for _ in range(STEPS):
            fields = [absorb * stencil(q, fwd) for q in fields]
        gridded = observe(fields, e)
        fields = [gridded[r] for r in range(share)]
        for _ in range(STEPS):
            fields = [stencil(absorb * p, adj) for p in fields]
        for r in range(share):
            ext[pl.ds(r * n, n), :] = fields[r]
            adj_stage[e, r] = fields[r][HALO:HALO + width]
            ag[e, m, r] = fields[r][HALO:HALO + width]
        for i, row in enumerate((HALO - 2, HALO - 1, HALO + width, HALO + width + 1)):
            v = ext[pl.ds(row, share, stride=n), :]
            edge_stage[e, i] = v
            agh[e, m, i] = v
        gathers = []
        for d in range(1, n_mem):
            gathers.append(send_mem(d, adj_stage.at[e], ag.at[e, m], ag_send.at[e, d], ag_recv.at[e, d]))
            gathers.append(send_mem(d, edge_stage.at[e], agh.at[e, m], e_send.at[e, d], e_recv.at[e, d]))
        for copy in gathers:
            copy.start()
        if e == 0:
            for side in (0, 1):
                recv_side(side, (6,))
        for copy in gathers:
            copy.wait_recv()
        half = levels * width
        whole = ag[e].reshape(rows * width, ny)
        for k in range(members):
            at = k * rows * width
            nxt[pl.ds(k * block, block), :] = (
                ensf[pl.ds(at, half), :] * whole[:half] + ensf[pl.ds(at + half, half), :] * whole[half:]
            )
        terms = []
        for i in range(4):
            a = agh[e, :, i].reshape(1, rows, ny)
            p = ens_halo[i // 2, i % 2].astype(F32).reshape(members, rows, ny) * a
            terms.append((p[:, :levels] + p[:, levels:]).reshape(kl, ny))

        def term_edges():
            parts = [terms[1], terms[2]]
            if e == 0:
                row0 = nxt[pl.ds(0, kl, stride=width), :]
                row1 = nxt[pl.ds(width - 1, kl, stride=width), :]
                parts.append(0.5 * terms[1] + 0.25 * (terms[0] + row0))
                parts.append(0.5 * terms[2] + 0.25 * (terms[3] + row1))
            return parts

        side = mix(nxt, 1, term_edges)

        def drain():
            for copy in copies + gathers:
                copy.wait_send()
            for s in (0, 1):
                @pl.when(has[1 - s])
                def _():
                    halo[s].wait_send()

        return side, drain

    def control_edges():
        for side in (0, 1):
            recv_side(side, (0,))
        return [ctl_halo[0], ctl_halo[1]]

    side, drain0 = evaluate(0, ctl, control_edges)
    outer = []
    for s in (0, 1):
        f = smooth_y(side[:, (2 + s) * ny:(3 + s) * ny])
        c = ctl_halo[s]
        inside = jnp.where(has[s], 1.0, 0.0).astype(F32)
        outer.append((c - step_length * (c + f)) * inside)
    for k in range(members):
        at = pl.ds(k * block, block)
        c = ctl[at, :]
        nxt[at, :] = c - step_length * (c + smooth_y(work[at, :]))
    _, drain1 = evaluate(1, nxt, lambda: outer)
    for k in range(members):
        at = pl.ds(k * block, block)
        out[at, :] = smooth_y(work[at, :])
    drain0()
    drain1()
    for s in (0, 1):
        @pl.when(has[1 - s])
        def _():
            for copy in first_msgs[s]:
                copy.wait_send()


def body(n_mem, n_tile, ensemble, control, level_loc, wind_speed, cell_codes, obs_cell, innovation, obs_sigma):
    members, rows, width, ny = ensemble.shape
    levels = control.shape[1]
    nobs = obs_cell.shape[0]
    share = rows // n_mem
    kl = members * levels
    block = levels * width
    n = width + 2 * HALO
    vmem = pltpu.VMEM
    dma = pltpu.SemaphoreType.DMA
    scratch = [
        vmem((members * rows * width, ny), F32),
        vmem((members * block, ny), F32),
        vmem((members * block, ny), F32),
        vmem((2, 2, block, block), BF16),
        vmem((2, 2, kl, kl), BF16),
        vmem((2, kl, ny), F32),
        vmem((2, kl, ny), F32),
        vmem((2, HALO, ny), jnp.int32),
        vmem((2, HALO, ny), F32),
        vmem((2, 1, nobs), jnp.int32),
        vmem((2, share, nobs), F32),
        vmem((2, share, nobs), F32),
        vmem((2, 2, members * rows, ny), BF16),
        vmem((2, 2, members * rows, ny), BF16),
        vmem((2, n_mem, share, width, ny), F32),
        vmem((2, n_mem, share, width, ny), F32),
        vmem((2, 2, share, HALO, ny), F32),
        vmem((2, 2, share, HALO, ny), F32),
        vmem((share * n, ny), F32),
        vmem((2, share, width, ny), F32),
        vmem((2, n_mem, share, width, ny), F32),
        vmem((2, 4, share, ny), F32),
        vmem((2, n_mem, 4, share, ny), F32),
        dma((2, 7)), dma((2, 7)),
        dma((2, n_mem)), dma((2, n_mem)),
        dma((2, 2)), dma((2, 2)),
        dma((2, n_mem)), dma((2, n_mem)),
        dma((2, n_mem)), dma((2, n_mem)),
    ]
    whole = pl.BlockSpec(memory_space=pltpu.VMEM)
    result = pl.pallas_call(
        functools.partial(kernel, n_mem, n_tile, members, levels, width, ny, nobs),
        out_shape=jax.ShapeDtypeStruct((members * block, ny), F32),
        in_specs=[whole] * 8,
        out_specs=whole,
        scratch_shapes=scratch,
        compiler_params=pltpu.CompilerParams(
            collective_id=0, has_side_effects=True, vmem_limit_bytes=48 << 20
        ),
    )(
        ensemble,
        control.reshape(members * block, ny),
        level_loc,
        wind_speed,
        cell_codes,
        obs_cell.reshape(1, nobs),
        innovation.reshape(n_mem, share, nobs),
        obs_sigma.reshape(n_mem, share, nobs),
    )
    return result.reshape(members, levels, width, ny)


def solution(mesh):
    placed = (
        P("mem", None, "tile", None),
        P("mem", None, "tile", None),
        P(),
        P("tile", None),
        P("tile", None),
        P("tile"),
        P(None, "tile"),
        P(None, "tile"),
    )
    return jax.shard_map(
        functools.partial(body, mesh.shape["mem"], mesh.shape["tile"]),
        mesh=mesh, in_specs=placed, out_specs=P("mem", None, "tile", None), check_vma=False,
    )
```

time: 209 us -> 47 us (0.22)
  waiting for transfers between devices: 80.5 us -> 0 us
  starting transfers between devices: 65.7 us -> 0 us
  Pallas kernels: 0 us -> 38.7 us
  other arithmetic: 16.1 us -> 0 us
  blocking collectives: 15.5 us -> 0 us
  between operations: 14.1 us -> 0.02 us
  matrix products: 6.61 us -> 0 us
    ppermute x26 -> x0, starting transfers between devices: 65.7 us -> none  [the longest x13 37.3 us: with_halo(): lax.ppermute(lax.slice_in_dim(block, block.shape[dim] - width, None, axis...]
    reduce_scatter x2 -> x0, waiting for transfers between devices: 45.5 us -> none  [evaluate(): lax.psum_scatter(partial_sum, 'mem', scatter_dimension=0, tiled=True)]
    pallas_call x0 -> x1, Pallas kernels: none -> 38.7 us  [body(): pl.pallas_call(functools.partial(kernel, n_mem, n_tile, members, levels,...]
    ppermute x26 -> x0, waiting for transfers between devices: 35 us -> none  [the longest x13 34.9 us: with_halo(): lax.ppermute(lax.slice_in_dim(block, 0, width, axis=dim), axis, backward)]
    all_gather x2 -> x0, blocking collectives: 15.5 us -> none  [evaluate(): adjoint_field = lax.all_gather(adjoint_field, 'mem', axis=0, tiled=True)]
    unnamed x18 -> x17, local copies, waits for them, and re-layouts: 1.02 us -> 7.87 us
    dot_general x4 -> x0, matrix products: 6.61 us -> none  [the longest x2 4.05 us: evaluate(): jnp.einsum('ml,klxy->kmxy', level_loc, weights, precision=highest)]
    scatter-add x2 -> x0, other arithmetic: 5.01 us -> none  [evaluate(): jnp.zeros((row_count, width_x * width_y), jnp.float32).at[:, obs_cell]]
  transfers between devices with their start and end apart: 28 -> 0, of which waited for: 14 -> 0; matrix products, arithmetic and copies ran while one was open for 2% -> 0% of each run, Pallas kernels for 0% -> 0%
where the time goes in v1:
time: 47 us; the launch traced here: 46.6 us
  Pallas kernels  38.7 us (82%)
  local copies, waits for them, and re-layouts  7.87 us (17%)
    pallas_call x1, Pallas kernels, body(): pl.pallas_call(functools.partial(kernel, n_mem, n_tile, members, levels,...  38.7 us
    unnamed x17, local copies, waits for them, and re-layouts  7.87 us

profile of v1, /device:TPU:1, one launch (start us, length us, event | category | flops | bytes accessed | tf_op | source)
XLA Modules:
  0.0 46.6 jit_solution(16331243608528892152)
XLA Ops:
  0.0 0.0 copy-start.7
  0.0 0.7 %copy-done.7 = s32[512]{0:T(512)S(1)} copy-done((s32[512]{0:T(512)S(1)}, s32[512]{0:T(512)}, u32[]{:S(2)}) %copy-start.7) | copy-done | bytes 2072
  0.7 0.0 copy-start
  0.7 1.2 %copy-done = bf16[8,32,16,128]{3,2,1,0:T(8,128)(2,1)S(1)} copy-done((bf16[8,32,16,128]{3,2,1,0:T(8,128)(2,1)S(1)}, bf16[8,32,16,128]{3,2,1,0:T(8,128)(2,1)}, u32[]{:S(2)}) %copy-start) | copy-done | bytes 1048600
  1.9 0.0 copy-start.1
  1.9 1.2 %copy-done.1 = f32[8,16,16,128]{3,2,1,0:T(8,128)S(1)} copy-done((f32[8,16,16,128]{3,2,1,0:T(8,128)S(1)}, f32[8,16,16,128]{3,2,1,0:T(8,128)}, u32[]{:S(2)}) %copy-start.1) | copy-done | bytes 1048600
  3.1 0.0 copy-start.2
  3.1 0.8 %copy-done.2 = f32[32,512]{1,0:T(8,128)S(1)} copy-done((f32[32,512]{1,0:T(8,128)S(1)}, f32[32,512]{1,0:T(8,128)}, u32[]{:S(2)}) %copy-start.2) | copy-done | bytes 65560
  4.0 0.0 copy-start.3
  4.0 0.8 %copy-done.3 = f32[32,512]{1,0:T(8,128)S(1)} copy-done((f32[32,512]{1,0:T(8,128)S(1)}, f32[32,512]{1,0:T(8,128)}, u32[]{:S(2)}) %copy-start.3) | copy-done | bytes 65560
  4.8 0.0 copy-start.4
  4.8 0.7 %copy-done.4 = f32[16,16]{1,0:T(8,128)S(1)} copy-done((f32[16,16]{1,0:T(8,128)S(1)}, f32[16,16]{1,0:T(8,128)}, u32[]{:S(2)}) %copy-start.4) | copy-done | bytes 1048
  5.5 0.0 copy-start.5
  5.5 0.7 %copy-done.5 = f32[16,128]{1,0:T(8,128)S(1)} copy-done((f32[16,128]{1,0:T(8,128)S(1)}, f32[16,128]{1,0:T(8,128)}, u32[]{:S(2)}) %copy-start.5) | copy-done | bytes 8216
  6.2 0.0 copy-start.6
  6.2 0.7 %copy-done.6 = s32[16,128]{1,0:T(8,128)S(1)} copy-done((s32[16,128]{1,0:T(8,128)S(1)}, s32[16,128]{1,0:T(8,128)}, u32[]{:S(2)}) %copy-start.6) | copy-done | bytes 8216
  6.9 38.7 %shard_map.82 = f32[2048,128]{1,0:T(8,128)S(1)} custom-call(bf16[8,32,16,128]{3,2,1,0:T(8,128)(2,1)S(1)} %copy-done, f32[2048,128]{1,0:T(8,128)S(1)} %bitcast.6, f32[16,16]{1,0:T(8,128)S(1)} %copy-done.4, f32[16,128]{1,0:T(8,128)S(1)} %copy-done.5, s32[16,128]{1,0:T(8,128)S(1)} %copy-done.6, s32[1,512]{1,0:T(1,128)S(1)} %bitcast.9, ...), custom_call_target="tpu_custom_call" | custom-call | tf_op jit(solution)/shard_map/pallas_call | solution.py:429
  45.6 1.0 %copy.10 = f32[8,16,16,128]{3,2,1,0:T(8,128)} copy(f32[8,16,16,128]{3,2,1,0:T(8,128)S(1)} %bitcast.5) | data formatting | bytes 2097152
Async XLA Ops:
  0.0 0.7 %copy-start.7 = (s32[512]{0:T(512)S(1)}, s32[512]{0:T(512)}, u32[]{:S(2)}) copy-start(s32[512]{0:T(512)} %param.13) | copy-start | bytes 6148
  0.7 1.2 %copy-start = (bf16[8,32,16,128]{3,2,1,0:T(8,128)(2,1)S(1)}, bf16[8,32,16,128]{3,2,1,0:T(8,128)(2,1)}, u32[]{:S(2)}) copy-start(bf16[8,32,16,128]{3,2,1,0:T(8,128)(2,1)} %ens.1) | copy-start | bytes 3145732
  1.9 1.2 %copy-start.1 = (f32[8,16,16,128]{3,2,1,0:T(8,128)S(1)}, f32[8,16,16,128]{3,2,1,0:T(8,128)}, u32[]{:S(2)}) copy-start(f32[8,16,16,128]{3,2,1,0:T(8,128)} %param.9) | copy-start | bytes 3145732
  3.1 0.8 %copy-start.2 = (f32[32,512]{1,0:T(8,128)S(1)}, f32[32,512]{1,0:T(8,128)}, u32[]{:S(2)}) copy-start(f32[32,512]{1,0:T(8,128)} %param.14) | copy-start | bytes 196612
  4.0 0.8 %copy-start.3 = (f32[32,512]{1,0:T(8,128)S(1)}, f32[32,512]{1,0:T(8,128)}, u32[]{:S(2)}) copy-start(f32[32,512]{1,0:T(8,128)} %param.15) | copy-start | bytes 196612
  4.8 0.7 %copy-start.4 = (f32[16,16]{1,0:T(8,128)S(1)}, f32[16,16]{1,0:T(8,128)}, u32[]{:S(2)}) copy-start(f32[16,16]{1,0:T(8,128)} %loc.1) | copy-start | bytes 3076
  5.5 0.7 %copy-start.5 = (f32[16,128]{1,0:T(8,128)S(1)}, f32[16,128]{1,0:T(8,128)}, u32[]{:S(2)}) copy-start(f32[16,128]{1,0:T(8,128)} %wind.1) | copy-start | bytes 24580
  6.2 0.7 %copy-start.6 = (s32[16,128]{1,0:T(8,128)S(1)}, s32[16,128]{1,0:T(8,128)}, u32[]{:S(2)}) copy-start(s32[16,128]{1,0:T(8,128)} %codes.1) | copy-start | bytes 24580

commit v2 on v1

--- a/solution.py
+++ b/solution.py
@@ -49,8 +49,9 @@
 
 def kernel(
     n_mem, n_tile, members, levels, width, ny, nobs,
-    ens, ctl, loc, wind, codes, cell, innov, sigma,
+    ens_hbm, ctl_hbm, loc_hbm, wind_hbm, codes_hbm, cell_hbm, innov_hbm, sigma_hbm,
     out,
+    ens, ctl, loc, wind, codes, cell, innov, sigma, in_sem,
     ensf, work, nxt, mats, small,
     ctl_stage, ctl_halo, codes_halo, wind_halo, cell_halo, innov_halo, sigma_halo,
     ens_stage, ens_halo,
@@ -79,6 +80,17 @@
     def _():
         tell((m, t + 1))
 
+    loads = [
+        pltpu.make_async_copy(src, dst, in_sem.at[i])
+        for i, (src, dst) in enumerate((
+            (ctl_hbm, ctl), (loc_hbm, loc), (ens_hbm, ens), (wind_hbm, wind), (codes_hbm, codes),
+            (cell_hbm, cell), (innov_hbm.at[m], innov), (sigma_hbm.at[m], sigma),
+        ))
+    ]
+    for load in loads:
+        load.start()
+    loads[0].wait()
+
     kl = members * levels
     ctl_stage[0] = ctl[pl.ds(width - 1, kl, stride=width), :]
     ctl_stage[1] = ctl[pl.ds(0, kl, stride=width), :]
@@ -98,11 +110,11 @@
     for side in (0, 1):
         pairs = [
             (ctl_stage.at[side], ctl_halo.at[side]),
-            (codes.at[near[side]], codes_halo.at[side]),
-            (wind.at[near[side]], wind_halo.at[side]),
-            (cell, cell_halo.at[side]),
-            (innov.at[m], innov_halo.at[side]),
-            (sigma.at[m], sigma_halo.at[side]),
+            (codes_hbm.at[near[side]], codes_halo.at[side]),
+            (wind_hbm.at[near[side]], wind_halo.at[side]),
+            (cell_hbm, cell_halo.at[side]),
+            (innov_hbm.at[m], innov_halo.at[side]),
+            (sigma_hbm.at[m], sigma_halo.at[side]),
             (ens_stage.at[side], ens_halo.at[side]),
         ]
         first_msgs.append(
@@ -138,6 +150,7 @@
             for e in (0, 1):
                 inc_halo[e, side] = jnp.zeros_like(inc_halo[e, side])
 
+    loads[1].wait()
     lo = loc[...]
     pick = (iota((block, levels), 0) >> xs == iota((block, levels), 1)).astype(F32)
     xr, xc = iota((block, block), 0) & (width - 1), iota((block, block), 1) & (width - 1)
@@ -220,7 +233,7 @@
         state = jnp.stack(field, axis=0)
         tiles = (
             (cell_halo[0], innov_halo[0], sigma_halo[0], 0, HALO, width - HALO),
-            (cell[...], innov[m], sigma[m], HALO, width, 0),
+            (cell[...], innov[...], sigma[...], HALO, width, 0),
             (cell_halo[1], innov_halo[1], sigma_halo[1], HALO + width, HALO, 0),
         )
         pieces = []
@@ -249,6 +262,8 @@
             at = pl.ds(k * block, block)
             work[at, :] = smooth_y(work[at, :])
         copies = []
+        if e == 0:
+            loads[2].wait()
         for d in list(range(1, n_mem)) + [0]:
             who = lax.rem(m + d, n_mem)
             r0 = who * share
@@ -268,12 +283,14 @@
                     ens[k].astype(F32).reshape(rows * width, ny)
                 )
             for i in (0, 1):
-                ens_stage[0, i] = ensf[pl.ds(width - 2 + i, members * rows, stride=width), :].astype(BF16)
+                ens_stage[0, i] = ensf[pl.ds(width - 1 - i, members * rows, stride=width), :].astype(BF16)
                 ens_stage[1, i] = ensf[pl.ds(i, members * rows, stride=width), :].astype(BF16)
             for side in (0, 1):
                 start_side(side, (6,))
             for side in (0, 1):
                 recv_side(side, (1, 2, 3, 4, 5))
+            for load in loads[3:]:
+                load.wait()
         for copy in copies:
             copy.wait_recv()
         total = part[e, 0]
@@ -307,19 +324,22 @@
             ext[pl.ds(r * n, n), :] = fields[r]
             adj_stage[e, r] = fields[r][HALO:HALO + width]
             ag[e, m, r] = fields[r][HALO:HALO + width]
-        for i, row in enumerate((HALO - 2, HALO - 1, HALO + width, HALO + width + 1)):
+        marks = (HALO - 1, HALO + width) + ((HALO - 2, HALO + width + 1) if e == 0 else ())
+        for i, row in enumerate(marks):
             v = ext[pl.ds(row, share, stride=n), :]
             edge_stage[e, i] = v
             agh[e, m, i] = v
-        gathers = []
+        gathers, fringes = [], []
+        lines = pl.ds(0, len(marks))
         for d in range(1, n_mem):
             gathers.append(send_mem(d, adj_stage.at[e], ag.at[e, m], ag_send.at[e, d], ag_recv.at[e, d]))
-            gathers.append(send_mem(d, edge_stage.at[e], agh.at[e, m], e_send.at[e, d], e_recv.at[e, d]))
-        for copy in gathers:
+            fringes.append(
+                send_mem(
+                    d, edge_stage.at[e, lines], agh.at[e, m, lines], e_send.at[e, d], e_recv.at[e, d]
+                )
+            )
+        for copy in gathers + fringes:
             copy.start()
-        if e == 0:
-            for side in (0, 1):
-                recv_side(side, (6,))
         for copy in gathers:
             copy.wait_recv()
         half = levels * width
@@ -329,25 +349,29 @@
             nxt[pl.ds(k * block, block), :] = (
                 ensf[pl.ds(at, half), :] * whole[:half] + ensf[pl.ds(at + half, half), :] * whole[half:]
             )
-        terms = []
-        for i in range(4):
-            a = agh[e, :, i].reshape(1, rows, ny)
-            p = ens_halo[i // 2, i % 2].astype(F32).reshape(members, rows, ny) * a
-            terms.append((p[:, :levels] + p[:, levels:]).reshape(kl, ny))
-
         def term_edges():
-            parts = [terms[1], terms[2]]
+            for copy in fringes:
+                copy.wait_recv()
+            if e == 0:
+                for side in (0, 1):
+                    recv_side(side, (6,))
+            terms = []
+            for i in range(len(marks)):
+                a = agh[e, :, i].reshape(1, rows, ny)
+                p = ens_halo[i % 2, i // 2].astype(F32).reshape(members, rows, ny) * a
+                terms.append((p[:, :levels] + p[:, levels:]).reshape(kl, ny))
+            parts = terms[:2]
             if e == 0:
                 row0 = nxt[pl.ds(0, kl, stride=width), :]
                 row1 = nxt[pl.ds(width - 1, kl, stride=width), :]
-                parts.append(0.5 * terms[1] + 0.25 * (terms[0] + row0))
-                parts.append(0.5 * terms[2] + 0.25 * (terms[3] + row1))
+                parts.append(0.5 * terms[0] + 0.25 * (terms[2] + row0))
+                parts.append(0.5 * terms[1] + 0.25 * (terms[3] + row1))
             return parts
 
         side = mix(nxt, 1, term_edges)
 
         def drain():
-            for copy in copies + gathers:
+            for copy in copies + gathers + fringes:
                 copy.wait_send()
             for s in (0, 1):
                 @pl.when(has[1 - s])
@@ -396,6 +420,15 @@
     vmem = pltpu.VMEM
     dma = pltpu.SemaphoreType.DMA
     scratch = [
+        vmem((members, rows, width, ny), BF16),
+        vmem((members * block, ny), F32),
+        vmem((levels, levels), F32),
+        vmem((width, ny), F32),
+        vmem((width, ny), jnp.int32),
+        vmem((1, nobs), jnp.int32),
+        vmem((share, nobs), F32),
+        vmem((share, nobs), F32),
+        dma((8,)),
         vmem((members * rows * width, ny), F32),
         vmem((members * block, ny), F32),
         vmem((members * block, ny), F32),
@@ -429,13 +462,13 @@
     result = pl.pallas_call(
         functools.partial(kernel, n_mem, n_tile, members, levels, width, ny, nobs),
         out_shape=jax.ShapeDtypeStruct((members * block, ny), F32),
-        in_specs=[whole] * 8,
+        in_specs=[pl.BlockSpec(memory_space=pltpu.HBM)] * 8,
         out_specs=whole,
         scratch_shapes=scratch,
         compiler_params=pltpu.CompilerParams(
             collective_id=0, has_side_effects=True, vmem_limit_bytes=48 << 20
         ),
-    )(
+    )(*(pltpu.with_memory_space_constraint(x, pltpu.HBM) for x in (
         ensemble,
         control.reshape(members * block, ny),
         level_loc,
@@ -444,7 +477,7 @@
         obs_cell.reshape(1, nobs),
         innovation.reshape(n_mem, share, nobs),
         obs_sigma.reshape(n_mem, share, nobs),
-    )
+    )))
     return result.reshape(members, levels, width, ny)
 
 

time: 47 us -> 39.4 us (0.84)
  local copies, waits for them, and re-layouts: 7.87 us -> 0.97 us
  Pallas kernels: 38.7 us -> 38.2 us
    unnamed x17 -> x1, local copies, waits for them, and re-layouts: 7.87 us -> 0.97 us
where the time goes in v2:
time: 39.4 us; the launch traced here: 39.2 us
  Pallas kernels  38.2 us (97%)
  local copies, waits for them, and re-layouts  0.97 us (2%)
    pallas_call x1, Pallas kernels, body(): pl.pallas_call(functools.partial(kernel, n_mem, n_tile, members, levels,...  38.2 us
    unnamed x1, local copies, waits for them, and re-layouts  0.97 us

profile of v2, /device:TPU:1, one launch (start us, length us, event | category | flops | bytes accessed | tf_op | source)
XLA Modules:
  0.0 39.2 jit_solution(9899473544586191897)
XLA Ops:
  0.0 38.2 %shard_map.82 = f32[2048,128]{1,0:T(8,128)S(1)} custom-call(bf16[8,32,16,128]{3,2,1,0:T(8,128)(2,1)} %ens_hbm.1, f32[2048,128]{1,0:T(8,128)} %bitcast.6, f32[16,16]{1,0:T(8,128)} %loc_hbm.1, f32[16,128]{1,0:T(8,128)} %wind_hbm.1, s32[16,128]{1,0:T(8,128)} %codes_hbm.1, s32[1,512]{1,0:T(1,128)} %bitcast.9, f32[4,8,512]{2,1,0:T(8,128)} %bitcast.7, ...), custom_call_target="tpu_custom_call" | custom-call | tf_op jit(solution)/shard_map/pallas_call | solution.py:462
  38.2 1.0 %copy.10 = f32[8,16,16,128]{3,2,1,0:T(8,128)} copy(f32[8,16,16,128]{3,2,1,0:T(8,128)S(1)} %bitcast.5) | data formatting | bytes 2097152

commit v3 on v2

--- a/solution.py
+++ b/solution.py
@@ -51,7 +51,7 @@
     n_mem, n_tile, members, levels, width, ny, nobs,
     ens_hbm, ctl_hbm, loc_hbm, wind_hbm, codes_hbm, cell_hbm, innov_hbm, sigma_hbm,
     out,
-    ens, ctl, loc, wind, codes, cell, innov, sigma, in_sem,
+    ens, ctl, loc, wind, codes, cell, innov, sigma, in_sem, hot,
     ensf, work, nxt, mats, small,
     ctl_stage, ctl_halo, codes_halo, wind_halo, cell_halo, innov_halo, sigma_halo,
     ens_stage, ens_halo,
@@ -64,6 +64,7 @@
     rows = V * levels
     share = rows // n_mem
     block = levels * width
+    kl = members * levels
     xs = log2(width)
 
     def tell(dev):
@@ -87,11 +88,34 @@
             (cell_hbm, cell), (innov_hbm.at[m], innov), (sigma_hbm.at[m], sigma),
         ))
     ]
-    for load in loads:
-        load.start()
+    for i in (1, 0, 2, 3, 4, 5, 6, 7):
+        loads[i].start()
+
+    loads[1].wait()
+    lo = loc[...]
+    pick = (iota((block, levels), 0) >> xs == iota((block, levels), 1)).astype(F32)
+    xr, xc = iota((block, block), 0) & (width - 1), iota((block, block), 1) & (width - 1)
+    near_x = jnp.where(xr == xc, 0.5, jnp.where(jnp.abs(xr - xc) == 1, 0.25, 0.0)).astype(F32)
+    ls = log2(levels)
+    pick2 = ((iota((kl, levels), 0) & (levels - 1)) == iota((kl, levels), 1)).astype(F32)
+    same_k = ((iota((kl, kl), 0) >> ls) == (iota((kl, kl), 1) >> ls)).astype(F32)
+
+    def nt(a, b):
+        return lax.dot_general(a, b, NT, precision=HIGHEST, preferred_element_type=F32)
+
+    for i in (0, 1):
+        def left(p):
+            return jnp.dot(p, lo, precision=HIGHEST, preferred_element_type=F32) if i == 0 else nt(p, lo)
+
+        hi, low = split(nt(left(pick), pick) * near_x)
+        mats[i, 0] = hi
+        mats[i, 1] = low
+        hi, low = split(nt(left(pick2), pick2) * same_k)
+        small[i, 0] = hi
+        small[i, 1] = low
+
     loads[0].wait()
 
-    kl = members * levels
     ctl_stage[0] = ctl[pl.ds(width - 1, kl, stride=width), :]
     ctl_stage[1] = ctl[pl.ds(0, kl, stride=width), :]
 
@@ -150,29 +174,6 @@
             for e in (0, 1):
                 inc_halo[e, side] = jnp.zeros_like(inc_halo[e, side])
 
-    loads[1].wait()
-    lo = loc[...]
-    pick = (iota((block, levels), 0) >> xs == iota((block, levels), 1)).astype(F32)
-    xr, xc = iota((block, block), 0) & (width - 1), iota((block, block), 1) & (width - 1)
-    near_x = jnp.where(xr == xc, 0.5, jnp.where(jnp.abs(xr - xc) == 1, 0.25, 0.0)).astype(F32)
-    ls = log2(levels)
-    pick2 = ((iota((kl, levels), 0) & (levels - 1)) == iota((kl, levels), 1)).astype(F32)
-    same_k = ((iota((kl, kl), 0) >> ls) == (iota((kl, kl), 1) >> ls)).astype(F32)
-
-    def nt(a, b):
-        return lax.dot_general(a, b, NT, precision=HIGHEST, preferred_element_type=F32)
-
-    for i in (0, 1):
-        def left(p):
-            return jnp.dot(p, lo, precision=HIGHEST, preferred_element_type=F32) if i == 0 else nt(p, lo)
-
-        hi, low = split(nt(left(pick), pick) * near_x)
-        mats[i, 0] = hi
-        mats[i, 1] = low
-        hi, low = split(nt(left(pick2), pick2) * same_k)
-        small[i, 0] = hi
-        small[i, 1] = low
-
     yi = iota((1, ny), 1)
     from_south = jnp.where(yi > 0, 0.25, 0.0).astype(F32)
     from_north = jnp.where(yi < ny - 1, 0.25, 0.0).astype(F32)
@@ -237,8 +238,8 @@
             (cell_halo[1], innov_halo[1], sigma_halo[1], HALO + width, HALO, 0),
         )
         pieces = []
-        for where, seen, dev, at, count, offset in tiles:
-            hot_y = (iota((ny, nobs), 0) == (where & (ny - 1))).astype(BF16)
+        for i, (where, seen, dev, at, count, offset) in enumerate(tiles):
+            hot_y = hot[i]
             hot_x = (iota((count, nobs), 0) == ((where >> log2(ny)) - offset)).astype(F32)
             part_state = state[:, at:at + count, :].reshape(share * count, ny)
             hi, low = split(part_state)
@@ -291,6 +292,8 @@
                 recv_side(side, (1, 2, 3, 4, 5))
             for load in loads[3:]:
                 load.wait()
+            for i, where in enumerate((cell_halo[0], cell[...], cell_halo[1])):
+                hot[i] = (iota((ny, nobs), 0) == (where & (ny - 1))).astype(BF16)
         for copy in copies:
             copy.wait_recv()
         total = part[e, 0]
@@ -324,21 +327,26 @@
             ext[pl.ds(r * n, n), :] = fields[r]
             adj_stage[e, r] = fields[r][HALO:HALO + width]
             ag[e, m, r] = fields[r][HALO:HALO + width]
+        gathers = [
+            send_mem(d, adj_stage.at[e], ag.at[e, m], ag_send.at[e, d], ag_recv.at[e, d])
+            for d in range(1, n_mem)
+        ]
+        for copy in gathers:
+            copy.start()
         marks = (HALO - 1, HALO + width) + ((HALO - 2, HALO + width + 1) if e == 0 else ())
         for i, row in enumerate(marks):
             v = ext[pl.ds(row, share, stride=n), :]
             edge_stage[e, i] = v
             agh[e, m, i] = v
-        gathers, fringes = [], []
+        fringes = []
         lines = pl.ds(0, len(marks))
         for d in range(1, n_mem):
-            gathers.append(send_mem(d, adj_stage.at[e], ag.at[e, m], ag_send.at[e, d], ag_recv.at[e, d]))
             fringes.append(
                 send_mem(
                     d, edge_stage.at[e, lines], agh.at[e, m, lines], e_send.at[e, d], e_recv.at[e, d]
                 )
             )
-        for copy in gathers + fringes:
+        for copy in fringes:
             copy.start()
         for copy in gathers:
             copy.wait_recv()
@@ -429,6 +437,7 @@
         vmem((share, nobs), F32),
         vmem((share, nobs), F32),
         dma((8,)),
+        vmem((3, ny, nobs), BF16),
         vmem((members * rows * width, ny), F32),
         vmem((members * block, ny), F32),
         vmem((members * block, ny), F32),

time: 39.4 us -> 39.6 us (level)
  no operation moved by 1% of the time
where the time goes in v3:
time: 39.6 us; the launch traced here: 39.4 us
  Pallas kernels  38.4 us (97%)
  local copies, waits for them, and re-layouts  0.97 us (2%)
    pallas_call x1, Pallas kernels, body(): pl.pallas_call(functools.partial(kernel, n_mem, n_tile, members, levels,...  38.4 us
    unnamed x1, local copies, waits for them, and re-layouts  0.97 us

profile of v3, /device:TPU:1, one launch (start us, length us, event | category | flops | bytes accessed | tf_op | source)
XLA Modules:
  0.0 39.4 jit_solution(5730039048555705928)
XLA Ops:
  0.0 38.4 %shard_map.82 = f32[2048,128]{1,0:T(8,128)S(1)} custom-call(bf16[8,32,16,128]{3,2,1,0:T(8,128)(2,1)} %ens_hbm.1, f32[2048,128]{1,0:T(8,128)} %bitcast.6, f32[16,16]{1,0:T(8,128)} %loc_hbm.1, f32[16,128]{1,0:T(8,128)} %wind_hbm.1, s32[16,128]{1,0:T(8,128)} %codes_hbm.1, s32[1,512]{1,0:T(1,128)} %bitcast.9, f32[4,8,512]{2,1,0:T(8,128)} %bitcast.7, ...), custom_call_target="tpu_custom_call" | custom-call | tf_op jit(solution)/shard_map/pallas_call | solution.py:471
  38.4 1.0 %copy.10 = f32[8,16,16,128]{3,2,1,0:T(8,128)} copy(f32[8,16,16,128]{3,2,1,0:T(8,128)S(1)} %bitcast.5) | data formatting | bytes 2097152

commit v4 on v2

--- a/solution.py
+++ b/solution.py
@@ -51,7 +51,7 @@
     n_mem, n_tile, members, levels, width, ny, nobs,
     ens_hbm, ctl_hbm, loc_hbm, wind_hbm, codes_hbm, cell_hbm, innov_hbm, sigma_hbm,
     out,
-    ens, ctl, loc, wind, codes, cell, innov, sigma, in_sem,
+    ens, ctl, loc, wind, codes, cell, innov, sigma, in_sem, hot,
     ensf, work, nxt, mats, small,
     ctl_stage, ctl_halo, codes_halo, wind_halo, cell_halo, innov_halo, sigma_halo,
     ens_stage, ens_halo,
@@ -64,6 +64,7 @@
     rows = V * levels
     share = rows // n_mem
     block = levels * width
+    kl = members * levels
     xs = log2(width)
 
     def tell(dev):
@@ -87,11 +88,11 @@
             (cell_hbm, cell), (innov_hbm.at[m], innov), (sigma_hbm.at[m], sigma),
         ))
     ]
-    for load in loads:
-        load.start()
+    for i in range(len(loads)):
+        loads[i].start()
+
     loads[0].wait()
 
-    kl = members * levels
     ctl_stage[0] = ctl[pl.ds(width - 1, kl, stride=width), :]
     ctl_stage[1] = ctl[pl.ds(0, kl, stride=width), :]
 
@@ -237,8 +238,8 @@
             (cell_halo[1], innov_halo[1], sigma_halo[1], HALO + width, HALO, 0),
         )
         pieces = []
-        for where, seen, dev, at, count, offset in tiles:
-            hot_y = (iota((ny, nobs), 0) == (where & (ny - 1))).astype(BF16)
+        for i, (where, seen, dev, at, count, offset) in enumerate(tiles):
+            hot_y = hot[i]
             hot_x = (iota((count, nobs), 0) == ((where >> log2(ny)) - offset)).astype(F32)
             part_state = state[:, at:at + count, :].reshape(share * count, ny)
             hi, low = split(part_state)
@@ -291,6 +292,8 @@
                 recv_side(side, (1, 2, 3, 4, 5))
             for load in loads[3:]:
                 load.wait()
+            for i, where in enumerate((cell_halo[0], cell[...], cell_halo[1])):
+                hot[i] = (iota((ny, nobs), 0) == (where & (ny - 1))).astype(BF16)
         for copy in copies:
             copy.wait_recv()
         total = part[e, 0]
@@ -324,21 +327,26 @@
             ext[pl.ds(r * n, n), :] = fields[r]
             adj_stage[e, r] = fields[r][HALO:HALO + width]
             ag[e, m, r] = fields[r][HALO:HALO + width]
+        gathers = [
+            send_mem(d, adj_stage.at[e], ag.at[e, m], ag_send.at[e, d], ag_recv.at[e, d])
+            for d in range(1, n_mem)
+        ]
+        for copy in gathers:
+            copy.start()
         marks = (HALO - 1, HALO + width) + ((HALO - 2, HALO + width + 1) if e == 0 else ())
         for i, row in enumerate(marks):
             v = ext[pl.ds(row, share, stride=n), :]
             edge_stage[e, i] = v
             agh[e, m, i] = v
-        gathers, fringes = [], []
+        fringes = []
         lines = pl.ds(0, len(marks))
         for d in range(1, n_mem):
-            gathers.append(send_mem(d, adj_stage.at[e], ag.at[e, m], ag_send.at[e, d], ag_recv.at[e, d]))
             fringes.append(
                 send_mem(
                     d, edge_stage.at[e, lines], agh.at[e, m, lines], e_send.at[e, d], e_recv.at[e, d]
                 )
             )
-        for copy in gathers + fringes:
+        for copy in fringes:
             copy.start()
         for copy in gathers:
             copy.wait_recv()
@@ -429,6 +437,7 @@
         vmem((share, nobs), F32),
         vmem((share, nobs), F32),
         dma((8,)),
+        vmem((3, ny, nobs), BF16),
         vmem((members * rows * width, ny), F32),
         vmem((members * block, ny), F32),
         vmem((members * block, ny), F32),

time: 39.4 us -> 39.2 us (level)
  no operation moved by 1% of the time
where the time goes in v4:
time: 39.2 us; the launch traced here: 39.1 us
  Pallas kernels  38.1 us (97%)
  local copies, waits for them, and re-layouts  0.97 us (2%)
    pallas_call x1, Pallas kernels, body(): pl.pallas_call(functools.partial(kernel, n_mem, n_tile, members, levels,...  38.1 us
    unnamed x1, local copies, waits for them, and re-layouts  0.97 us

profile of v4, /device:TPU:1, one launch (start us, length us, event | category | flops | bytes accessed | tf_op | source)
XLA Modules:
  0.0 39.1 jit_solution(7312690383159149213)
XLA Ops:
  0.0 38.1 %shard_map.82 = f32[2048,128]{1,0:T(8,128)S(1)} custom-call(bf16[8,32,16,128]{3,2,1,0:T(8,128)(2,1)} %ens_hbm.1, f32[2048,128]{1,0:T(8,128)} %bitcast.6, f32[16,16]{1,0:T(8,128)} %loc_hbm.1, f32[16,128]{1,0:T(8,128)} %wind_hbm.1, s32[16,128]{1,0:T(8,128)} %codes_hbm.1, s32[1,512]{1,0:T(1,128)} %bitcast.9, f32[4,8,512]{2,1,0:T(8,128)} %bitcast.7, ...), custom_call_target="tpu_custom_call" | custom-call | tf_op jit(solution)/shard_map/pallas_call | solution.py:471
  38.1 1.0 %copy.10 = f32[8,16,16,128]{3,2,1,0:T(8,128)} copy(f32[8,16,16,128]{3,2,1,0:T(8,128)S(1)} %bitcast.5) | data formatting | bytes 2097152
